TPU v7x, 32 devices: a whole 2x2x4 slice. The times are simulated.
32 devices in a mesh: band: 8 (over z, y), mode: 4 (over x, core).
Axes of the slice: x: 2, y: 2, z: 4, core: 2. Of those that a mesh axis runs over, the one named last changes fastest.
Arguments:
- velocity: bfloat16 [1, 8192, 1024], P(None, ('band', 'mode')), may hold values from -6 to 6
- radiation_modes: bfloat16 [8192, 1024], P('band', 'mode'), may hold values from -0.125 to 0.125
- resistance: float32 [8, 1024, 1024], P('band', None, 'mode'), as said below
- mode_ranks: int32 [8], P('band'), may hold values from 128 to 1024, as said below
- freq_table: int32 [512], replicated, may hold values from 0 to 511, each once
Outputs:
- adjoint_force: bfloat16 [1, 8192, 1024], P(None, ('band', 'mode'))
Inputs may be any that keep to these rules, and one draw needn't show every extreme that they name: `resistance`: each band's matrix is symmetric. `mode_ranks`: the ranks never fall with the band index; the first band keeps 1024 // 8 modes and the last 1024.
All inputs are finite; a program needn't handle non-finite values.
Results may differ from a plain program's by a relative error of at most 0.015.
Values may be sent and summed in bfloat16 or wider, within the bound.
A program may use at most 64 MiB of HBM per device.

v0:
```python
import math
import jax
import jax.numpy as jnp
from jax import lax
from jax.sharding import PartitionSpec as P


def make_table(freq_table, step_count):
    times = jnp.arange(step_count, dtype=jnp.int32)
    phases = times[:, None] * freq_table[None, :] % step_count
    angles = phases.astype(jnp.float32) * (2.0 * math.pi / step_count)
    norming = 1.0 / math.sqrt(step_count)
    table = jnp.stack([jnp.cos(angles), -jnp.sin(angles)], axis=1) * norming
    return table.astype(jnp.bfloat16)


def add_sources(received):
    return jnp.sum(received, axis=0)


def per_device(velocity, radiation_modes, resistance, mode_ranks, freq_table):
    step_count = velocity.shape[2]
    mode_cols = radiation_modes.shape[1]
    dft_table = make_table(freq_table, step_count)
    spectra = jnp.einsum(
        "wpt,tcf->wpcf", velocity, dft_table, preferred_element_type=jnp.float32
    ).astype(jnp.bfloat16)
    partial_value = jnp.einsum(
        "wpcf,pr->wrcf",
        lax.all_gather(spectra, "mode", axis=1, tiled=True),
        radiation_modes,
        preferred_element_type=jnp.float32,
    )
    coefficients = add_sources(
        lax.all_to_all(
            partial_value[None].astype(jnp.bfloat16),
            "band",
            split_axis=4,
            concat_axis=0,
            tiled=True,
        ).astype(jnp.float32)
    )
    offset = lax.axis_index("mode") * mode_cols
    rank_here = mode_ranks[0]
    kept_mask = (offset + jnp.arange(mode_cols, dtype=jnp.int32) < rank_here).astype(jnp.float32)
    kept_mask = kept_mask[None, :, None, None]
    coefficients = coefficients * kept_mask
    matrix = resistance[0]
    partial_terms = jnp.einsum(
        "ij,wjcf->wicf", matrix, coefficients, precision=lax.Precision.HIGHEST
    )
    forcing = lax.psum_scatter(
        partial_terms.astype(jnp.bfloat16), "mode", scatter_dimension=1, tiled=True
    ).astype(jnp.float32)
    forcing = (2.0 * forcing * kept_mask).astype(jnp.bfloat16)
    collected = lax.all_gather(forcing, "mode", axis=1, tiled=True)
    collected = lax.all_gather(collected, "band", axis=3, tiled=True)
    own_basis = lax.all_to_all(radiation_modes, "mode", split_axis=0, concat_axis=1, tiled=True)
    surface_force = jnp.einsum(
        "pr,wrcf->wpcf", own_basis, collected, preferred_element_type=jnp.float32
    ).astype(jnp.bfloat16)
    history = jnp.einsum(
        "wpcf,tcf->wpt", surface_force, dft_table, preferred_element_type=jnp.float32
    )
    return history.astype(jnp.bfloat16)


def solution(mesh):
    placed = (
        P(None, ("band", "mode"), None),
        P("band", "mode"),
        P("band", None, "mode"),
        P("band"),
        P(),
    )
    return jax.shard_map(
        per_device,
        mesh=mesh,
        in_specs=placed,
        out_specs=P(None, ("band", "mode"), None),
        check_vma=False,
    )
```

profile of v0, /device:TPU:0, one launch (start us, length us, event | category | flops | bytes accessed | tf_op | source)
XLA Modules:
  0.0 158.5 jit_solution(3879735066893673971)
XLA Ops:
  6.5 9.1 %fusion.21 = (f32[1024,1,512]{0,2,1:T(8,128)S(1)}, f32[1024,1,512]{0,2,1:T(8,128)S(1)}) fusion(s32[512]{0:T(512)} %param.9), kind=kLoop, calls=%fused_computation.27 | loop fusion | flops 7864320 | bytes 4196352 | tf_op jit(solution)/shard_map/cos | solution.py:13
  15.7 1.3 copy-done.1
  17.0 0.6 copy-done.2
  17.7 1.6 fusion.13
  19.2 0.0 all-gather.6.cloned.1.call-update
  19.2 25.7 %all-gather.6.cloned.1.call-done = bf16[1024,2,512]{0,2,1:T(8,128)(2,1)} async-done(((bf16[256,2,512]{0,2,1:T(8,128)(2,1)}), bf16[1024,2,512]{0,2,1:T(8,128)(2,1)}) %all-gather.6.cloned.1.call-update) | async-done | bytes 2097168 | tf_op jit(solution)/shard_map/all_gather | solution.py:30
  44.9 2.3 %fusion.14 = bf16[1,1,256,2,512]{2,4,3,1,0:T(8,128)(2,1)S(1)} fusion(bf16[1024,2,512]{0,2,1:T(8,128)(2,1)} %all-gather.6.cloned.1.call-done, bf16[1024,256]{1,0:T(8,128)(2,1)S(1)} %copy-done.3), kind=kOutput, calls=%fused_computation.20 | convolution fusion | flops 537133056 | bytes 3145728 | tf_op jit(solution)/shard_map/wpcf,pr->wrcf/dot_general | solution.py:28
  47.2 1.3 copy.16
  48.6 5.5 %all-to-all-start = ((bf16[1,1,256,2,512]{2,3,1,0,4:T(2,128)(2,1)}), bf16[1,1,256,2,512]{2,3,1,0,4:T(2,128)(2,1)S(1)}, u32[]{:S(2)}, u32[]{:S(2)}) async-start(bf16[1,1,256,2,512]{2,3,1,0,4:T(2,128)(2,1)} %copy.16), calls=%async_computation | async-start | bytes 1048576 | tf_op jit(solution)/shard_map/all_to_all | solution.py:35
  54.1 0.2 reduce-scatter.2.cloned.1.call-start
  55.0 14.0 %all-to-all-done = bf16[1,1,256,2,512]{2,3,1,0,4:T(2,128)(2,1)S(1)} async-done(((bf16[1,1,256,2,512]{2,3,1,0,4:T(2,128)(2,1)}), bf16[1,1,256,2,512]{2,3,1,0,4:T(2,128)(2,1)S(1)}, u32[]{:S(2)}, u32[]{:S(2)}) %all-to-all-start) | async-done | bytes 524320 | tf_op jit(solution)/shard_map/all_to_all | solution.py:35
  69.0 0.5 convert_reduce_fusion
  69.5 1.9 %fusion.19 = bf16[1,1024,2,64]{1,3,2,0:T(8,128)(2,1)} fusion(f32[1,1024,256]{2,1,0:T(8,128)S(1)} %copy-done, f32[256,2,64]{0,1,2:T(2,128)S(1)} %convert_reduce_fusion, f32[256]{0:T(256)S(1)} %fusion.30), kind=kOutput, calls=%fused_computation.24 | convolution fusion | flops 402817024 | bytes 1442816 | tf_op jit(solution)/shard_map/ij,wjcf->wicf/dot_general | solution.py:49
  71.4 0.0 reduce-scatter.2.cloned.1.call-update
  71.4 0.0 all-gather.4.cloned.1.call-start
  71.5 18.3 %reduce-scatter.2.cloned.1.call-done = bf16[1,256,2,64]{1,3,2,0:T(8,128)(2,1)} async-done(((bf16[1,1024,2,64]{1,3,2,0:T(8,128)(2,1)}), bf16[1,256,2,64]{1,3,2,0:T(8,128)(2,1)}) %reduce-scatter.2.cloned.1.call-update) | async-done | bytes 65552 | tf_op jit(solution)/shard_map/reduce_scatter | solution.py:52
  89.7 0.9 multiply_convert_fusion
  90.6 6.2 %all_gather.10 = bf16[1,1024,2,64]{1,3,2,0:T(8,128)(2,1)} all-gather(bf16[1,256,2,64]{1,3,2,0:T(8,128)(2,1)S(1)} %multiply_convert_fusion), channel_id=1, replica_groups=mesh['band'=8,'mode'=4] {'mode'}, dimensions={1}, use_global_device_ids=true | all-gather | bytes 327680 | tf_op jit(solution)/shard_map/all_gather | solution.py:56
  96.8 0.0 all-gather.4.cloned.1.call-update
  96.8 11.2 %all_to_all.28 = bf16[4,256,256]{2,1,0:T(8,128)(2,1)S(1)} all-to-all(bf16[4,256,256]{2,1,0:T(8,128)(2,1)S(1)} %bitcast.57), channel_id=1, replica_groups=mesh['band'=8,'mode'=4] {'mode'}, dimensions={0} | all-to-all | bytes 1048576 | tf_op jit(solution)/shard_map/all_to_all | solution.py:58
  108.1 0.4 copy.18
  108.5 0.4 reshape.162
  108.8 37.2 %all-gather.4.cloned.1.call-done = bf16[1,1024,2,512]{1,3,2,0:T(8,128)(2,1)} async-done(((bf16[1,1024,2,64]{1,3,2,0:T(8,128)(2,1)}), bf16[1,1024,2,512]{1,3,2,0:T(8,128)(2,1)}) %all-gather.4.cloned.1.call-update) | async-done | bytes 2097168 | tf_op jit(solution)/shard_map/all_gather | solution.py:57
  146.1 5.9 %fusion.18 = bf16[1,256,1024]{2,1,0:T(8,128)(2,1)} fusion(bf16[256,1024,1]{1,0,2:T(8,128)(2,1)S(1)} %reshape.162, bf16[1,1024,2,512]{1,3,2,0:T(8,128)(2,1)} %all-gather.4.cloned.1.call-done, f32[1024,1,512]{0,2,1:T(8,128)} %copy-done.2, f32[1024,1,512]{0,2,1:T(8,128)} %copy-done.1), kind=kOutput, calls=%fused_computation.22 | convolution fusion | flops 1077411840 | bytes 7340032 | tf_op jit(solution)/shard_map/wpcf,tcf->wpt/dot_general | solution.py:62
  (11 shorter events, 0.0 us)
Async XLA Ops:
  6.5 62.9 %copy-start = (f32[1,1024,256]{2,1,0:T(8,128)S(1)}, f32[1,1024,256]{2,1,0:T(8,128)}, u32[]{:S(2)}) copy-start(f32[1,1024,256]{2,1,0:T(8,128)} %param.7) | copy-start | bytes 3145732
  6.5 11.1 %copy-start.4 = (bf16[1,256,1024]{2,1,0:T(8,128)(2,1)S(1)}, bf16[1,256,1024]{2,1,0:T(8,128)(2,1)}, u32[]{:S(2)}) copy-start(bf16[1,256,1024]{2,1,0:T(8,128)(2,1)} %param.5) | copy-start | bytes 1572868
  6.5 38.4 %all-gather.6.cloned.1.call-start = ((), (), s32[]{:S(2)}) async-start(), calls=%async_computation.5 | async-start | bytes 2621440 | tf_op jit(solution)/shard_map/all_gather | solution.py:30
  15.7 1.3 copy-start.1
  15.7 1.9 %copy-start.2 = (f32[1024,1,512]{0,2,1:T(8,128)}, f32[1024,1,512]{0,2,1:T(8,128)S(1)}, u32[]{:S(2)}) copy-start(f32[1024,1,512]{0,2,1:T(8,128)S(1)} %get-tuple-element.6) | copy-start | bytes 6291460
  17.7 27.3 %copy-start.3 = (bf16[1024,256]{1,0:T(8,128)(2,1)S(1)}, bf16[1024,256]{1,0:T(8,128)(2,1)}, u32[]{:S(2)}) copy-start(bf16[1024,256]{1,0:T(8,128)(2,1)} %param.6) | copy-start | bytes 1572868
  48.6 20.4 %all-to-all-start = ((bf16[1,1,256,2,512]{2,3,1,0,4:T(2,128)(2,1)}), bf16[1,1,256,2,512]{2,3,1,0,4:T(2,128)(2,1)S(1)}, u32[]{:S(2)}, u32[]{:S(2)}) async-start(bf16[1,1,256,2,512]{2,3,1,0,4:T(2,128)(2,1)} %copy.16), calls=%async_computation | async-start | bytes 1048576 | tf_op jit(solution)/shard_map/all_to_all | solution.py:35
  54.1 35.7 %reduce-scatter.2.cloned.1.call-start = ((), (), s32[]{:S(2)}) async-start(), calls=%async_computation.3 | async-start | bytes 327680 | tf_op jit(solution)/shard_map/reduce_scatter | solution.py:52
  71.4 74.7 %all-gather.4.cloned.1.call-start = ((), (), s32[]{:S(2)}) async-start(), calls=%async_computation.4 | async-start | bytes 2359296 | tf_op jit(solution)/shard_map/all_gather | solution.py:57
Sparse Core Ops, SparseCore 0:
  19.4 25.5 all-gather.5
  71.5 18.1 reduce-scatter.1
  97.0 49.0 all-gather.3
where the time goes:
time: 159 us
  waiting for transfers between devices  95.3 us (60%)
  blocking collectives  17.4 us (11%)
  between operations  13.8 us (9%)
  matrix products  11.7 us (7%)
  other arithmetic  10.5 us (7%)
  starting transfers between devices  5.78 us (4%)
  local copies, waits for them, and re-layouts  4.06 us (3%)
    all_gather x1, waiting for transfers between devices, per_device(): collected = lax.all_gather(collected, 'band', axis=3, tiled=True)  37.2 us
    all_gather x1, waiting for transfers between devices, per_device(): lax.all_gather(spectra, 'mode', axis=1, tiled=True)  25.7 us
    reduce_scatter x1, waiting for transfers between devices, per_device(): lax.psum_scatter(partial_terms.astype(jnp.bfloat16), 'mode', scatter_dime...  18.3 us
    all_to_all x1, waiting for transfers between devices, per_device(): lax.all_to_all(partial_value[None].astype(jnp.bfloat16), 'band', split_ax...  14 us
    all_to_all x1, blocking collectives, per_device(): lax.all_to_all(radiation_modes, 'mode', split_axis=0, concat_axis=1, tile...  11.2 us
    cos x1, other arithmetic, make_table(): table = jnp.stack([jnp.cos(angles), -jnp.sin(angles)], axis=1) * norming  9.14 us
    all_gather x1, blocking collectives, per_device(): collected = lax.all_gather(forcing, 'mode', axis=1, tiled=True)  6.23 us
    dot_general x1, matrix products, per_device(): jnp.einsum('wpcf,tcf->wpt', surface_force, dft_table, preferred_element_t...  5.95 us
  transfers between devices with their start and end apart: 4, of which 4 were waited for; matrix products, arithmetic and copies ran while one was open for 0% of the time, Pallas kernels for 0%

commit v1 on v0

--- a/solution.py
+++ b/solution.py
@@ -3,6 +3,22 @@
 import jax.numpy as jnp
 from jax import lax
 from jax.sharding import PartitionSpec as P
+
+
+def product_in_turn(value, axis, dim, term):
+    size, index, extent = (lax.axis_size(axis), lax.axis_index(axis), value.shape[dim])
+    forward = [(i, (i + 1) % size) for i in range(size)]
+    behind = [(i, (i - 1) % size) for i in range(size)]
+    middle = size // 2
+    from_left = from_right = value
+    so_far = term(value, index * extent)
+    for step in range(1, middle + 1):
+        from_left = lax.ppermute(from_left, axis, forward)
+        if step < size - middle:
+            from_right = lax.ppermute(from_right, axis, behind)
+            so_far = so_far + term(from_right, (index + step) % size * extent)
+        so_far = so_far + term(from_left, (index - step) % size * extent)
+    return so_far
 
 
 def make_table(freq_table, step_count):
@@ -25,11 +41,16 @@
     spectra = jnp.einsum(
         "wpt,tcf->wpcf", velocity, dft_table, preferred_element_type=jnp.float32
     ).astype(jnp.bfloat16)
-    partial_value = jnp.einsum(
-        "wpcf,pr->wrcf",
-        lax.all_gather(spectra, "mode", axis=1, tiled=True),
-        radiation_modes,
-        preferred_element_type=jnp.float32,
+    partial_value = product_in_turn(
+        spectra,
+        "mode",
+        1,
+        lambda shard, offset_2: jnp.einsum(
+            "wpcf,pr->wrcf",
+            shard,
+            lax.dynamic_slice_in_dim(radiation_modes, offset_2, shard.shape[1], axis=0),
+            preferred_element_type=jnp.float32,
+        ),
     )
     coefficients = add_sources(
         lax.all_to_all(

time: 159 us -> 152 us (0.956)
  waiting for transfers between devices: 95.3 us -> 84.3 us
  starting transfers between devices: 5.78 us -> 12.6 us
  matrix products: 11.7 us -> 10 us
    all_gather x1 -> x0, waiting for transfers between devices: 25.7 us -> none  [per_device(): lax.all_gather(spectra, 'mode', axis=1, tiled=True)]
    ppermute x0 -> x3, waiting for transfers between devices: none -> 14.9 us  [the longest x2 14.9 us: product_in_turn(): from_left = lax.ppermute(from_left, axis, forward)]
    ppermute x0 -> x3, starting transfers between devices: none -> 4.93 us  [the longest x2 3.01 us: product_in_turn(): from_left = lax.ppermute(from_left, axis, forward)]
    all_to_all x1, starting transfers between devices: 5.52 us -> 7.46 us  [per_device(): lax.all_to_all(partial_value[None].astype(jnp.bfloat16), 'band', split_ax...]
  transfers between devices with their start and end apart: 4 -> 6, of which waited for: 4 -> 5; matrix products, arithmetic and copies ran while one was open for 0% -> 1% of each run, Pallas kernels for 0% -> 0%
where the time goes in v1:
time: 152 us
  waiting for transfers between devices  84.3 us (55%)
  blocking collectives  17.4 us (11%)
  between operations  14.2 us (9%)
  starting transfers between devices  12.6 us (8%)
  other arithmetic  10.1 us (7%)
  matrix products  10 us (7%)
  local copies, waits for them, and re-layouts  3.13 us (2%)
    all_gather x1, waiting for transfers between devices, per_device(): collected = lax.all_gather(collected, 'band', axis=3, tiled=True)  37.2 us
    reduce_scatter x1, waiting for transfers between devices, per_device(): lax.psum_scatter(partial_terms.astype(jnp.bfloat16), 'mode', scatter_dime...  18.3 us
    ppermute x2, waiting for transfers between devices, product_in_turn(): from_left = lax.ppermute(from_left, axis, forward)  14.9 us
    all_to_all x1, waiting for transfers between devices, per_device(): lax.all_to_all(partial_value[None].astype(jnp.bfloat16), 'band', split_ax...  13.8 us
    all_to_all x1, blocking collectives, per_device(): lax.all_to_all(radiation_modes, 'mode', split_axis=0, concat_axis=1, tile...  11.2 us
    cos x1, other arithmetic, make_table(): table = jnp.stack([jnp.cos(angles), -jnp.sin(angles)], axis=1) * norming  9.14 us
    all_to_all x1, starting transfers between devices, per_device(): lax.all_to_all(partial_value[None].astype(jnp.bfloat16), 'band', split_ax...  7.46 us
    all_gather x1, blocking collectives, per_device(): collected = lax.all_gather(forcing, 'mode', axis=1, tiled=True)  6.23 us
  transfers between devices with their start and end apart: 6, of which 5 were waited for; matrix products, arithmetic and copies ran while one was open for 1% of the time, Pallas kernels for 0%

profile of v1, /device:TPU:0, one launch (start us, length us, event | category | flops | bytes accessed | tf_op | source)
XLA Modules:
  0.0 151.8 jit_solution(3906408760266521209)
XLA Ops:
  6.5 9.1 %fusion.21 = (f32[1024,1,512]{0,2,1:T(8,128)S(1)}, f32[1024,1,512]{0,2,1:T(8,128)S(1)}) fusion(s32[512]{0:T(512)} %param.9), kind=kLoop, calls=%fused_computation.29 | loop fusion | flops 7864320 | bytes 4196352 | tf_op jit(solution)/shard_map/cos | solution.py:29
  15.7 0.8 convolution_convert_fusion
  16.5 0.5 copy-done.2
  17.0 0.6 copy-done.3
  17.6 0.5 collective-permute-start.1
  18.1 1.9 %collective-permute-start = (bf16[1,256,2,512]{1,3,2,0:T(8,128)(2,1)S(1)}, bf16[1,256,2,512]{1,3,2,0:T(8,128)(2,1)S(1)}, u32[]{:S(2)}, u32[]{:S(2)}) collective-permute-start(bf16[1,256,2,512]{1,3,2,0:T(8,128)(2,1)S(1)} %bitcast.81), channel_id=1, source_target_pairs={{0,3},{1,0},{2,1},{3,2},{4,7},{5,4},{6,5},{7,6},{8,11},{9,8},{10,9... | collective-permute-start | bytes 1572872 | tf_op jit(solution)/shard_map/ppermute | solution.py:18
  20.1 0.3 fusion.27
  20.4 9.5 %collective-permute-done.1 = bf16[1,256,2,512]{1,3,2,0:T(8,128)(2,1)S(1)} collective-permute-done((bf16[1,256,2,512]{1,3,2,0:T(8,128)(2,1)S(1)}, bf16[1,256,2,512]{1,3,2,0:T(8,128)(2,1)S(1)}, u32[]{:S(2)}, u32[]{:S(2)}) %collective-permute-start.1) | collective-permute-done | bytes 524320 | tf_op jit(solution)/shard_map/ppermute | solution.py:16
  29.9 2.5 %collective-permute-start.2 = (bf16[1,256,2,512]{1,3,2,0:T(8,128)(2,1)S(1)}, bf16[1,256,2,512]{1,3,2,0:T(8,128)(2,1)S(1)}, u32[]{:S(2)}, u32[]{:S(2)}) collective-permute-start(bf16[1,256,2,512]{1,3,2,0:T(8,128)(2,1)S(1)} %collective-permute-done.1), channel_id=1, source_target_pairs={{0,1},{1,2},{2,3},{3,0},{4,5},{5,6},{6,7},{7,4},{8,9},{9,10},{10,1... | collective-permute-start | bytes 1572872 | tf_op jit(solution)/shard_map/ppermute | solution.py:16
  32.5 0.4 convolution_add_fusion.2
  32.8 0.4 convolution_add_fusion.1
  33.2 5.4 %collective-permute-done.2 = bf16[1,256,2,512]{1,3,2,0:T(8,128)(2,1)S(1)} collective-permute-done((bf16[1,256,2,512]{1,3,2,0:T(8,128)(2,1)S(1)}, bf16[1,256,2,512]{1,3,2,0:T(8,128)(2,1)S(1)}, u32[]{:S(2)}, u32[]{:S(2)}) %collective-permute-start.2) | collective-permute-done | bytes 524320 | tf_op jit(solution)/shard_map/ppermute | solution.py:16
  38.9 1.1 copy.37
  40.0 7.5 %all-to-all-start = ((bf16[1,1,256,2,512]{2,3,1,0,4:T(2,128)(2,1)}), bf16[1,1,256,2,512]{2,3,1,0,4:T(2,128)(2,1)S(1)}, u32[]{:S(2)}, u32[]{:S(2)}) async-start(bf16[1,1,256,2,512]{2,3,1,0,4:T(2,128)(2,1)} %copy.37), calls=%async_computation | async-start | bytes 1048576 | tf_op jit(solution)/shard_map/all_to_all | solution.py:56
  48.3 13.8 %all-to-all-done = bf16[1,1,256,2,512]{2,3,1,0,4:T(2,128)(2,1)S(1)} async-done(((bf16[1,1,256,2,512]{2,3,1,0,4:T(2,128)(2,1)}), bf16[1,1,256,2,512]{2,3,1,0,4:T(2,128)(2,1)S(1)}, u32[]{:S(2)}, u32[]{:S(2)}) %all-to-all-start) | async-done | bytes 524320 | tf_op jit(solution)/shard_map/all_to_all | solution.py:56
  62.4 1.9 %fusion.19 = bf16[1,1024,2,64]{1,3,2,0:T(8,128)(2,1)} fusion(f32[1,1024,256]{2,1,0:T(8,128)S(1)} %copy-done, f32[256,2,64]{0,2,1:T(8,128)S(1)} %convert_reduce_fusion, f32[256]{0:T(256)S(1)} %fusion.43), kind=kOutput, calls=%fused_computation.26 | convolution fusion | flops 402817024 | bytes 1442816 | tf_op jit(solution)/shard_map/ij,wjcf->wicf/dot_general | solution.py:70
  64.4 18.3 %reduce-scatter.2.cloned.1.call-done = bf16[1,256,2,64]{1,3,2,0:T(8,128)(2,1)} async-done(((bf16[1,1024,2,64]{1,3,2,0:T(8,128)(2,1)}), bf16[1,256,2,64]{1,3,2,0:T(8,128)(2,1)}) %reduce-scatter.2.cloned.1.call-update) | async-done | bytes 65552 | tf_op jit(solution)/shard_map/reduce_scatter | solution.py:73
  82.6 0.9 multiply_convert_fusion
  83.5 6.2 %all_gather.6 = bf16[1,1024,2,64]{1,3,2,0:T(8,128)(2,1)} all-gather(bf16[1,256,2,64]{1,3,2,0:T(8,128)(2,1)S(1)} %multiply_convert_fusion), channel_id=1, replica_groups=mesh['band'=8,'mode'=4] {'mode'}, dimensions={1}, use_global_device_ids=true | all-gather | bytes 327680 | tf_op jit(solution)/shard_map/all_gather | solution.py:77
  89.7 11.2 %all_to_all.28 = bf16[4,256,256]{2,1,0:T(8,128)(2,1)S(1)} all-to-all(bf16[4,256,256]{2,1,0:T(8,128)(2,1)S(1)} %bitcast.77), channel_id=1, replica_groups=mesh['band'=8,'mode'=4] {'mode'}, dimensions={0} | all-to-all | bytes 1048576 | tf_op jit(solution)/shard_map/all_to_all | solution.py:79
  101.0 0.4 copy.39
  101.4 0.4 reshape.186
  101.7 37.2 %all-gather.2.cloned.1.call-done = bf16[1,1024,2,512]{1,3,2,0:T(8,128)(2,1)} async-done(((bf16[1,1024,2,64]{1,3,2,0:T(8,128)(2,1)}), bf16[1,1024,2,512]{1,3,2,0:T(8,128)(2,1)}) %all-gather.2.cloned.1.call-update) | async-done | bytes 2097168 | tf_op jit(solution)/shard_map/all_gather | solution.py:78
  139.0 5.9 %fusion.18 = bf16[1,256,1024]{2,1,0:T(8,128)(2,1)} fusion(bf16[256,1024,1]{1,0,2:T(8,128)(2,1)S(1)} %reshape.186, bf16[1,1024,2,512]{1,3,2,0:T(8,128)(2,1)} %all-gather.2.cloned.1.call-done, f32[1024,1,512]{0,2,1:T(8,128)} %copy-done.3, f32[1024,1,512]{0,2,1:T(8,128)} %copy-done.2), kind=kOutput, calls=%fused_computation.24 | convolution fusion | flops 1077411840 | bytes 7340032 | tf_op jit(solution)/shard_map/wpcf,tcf->wpt/dot_general | solution.py:83
  (18 shorter events, 0.8 us)
Async XLA Ops:
  6.5 55.8 %copy-start = (f32[1,1024,256]{2,1,0:T(8,128)S(1)}, f32[1,1024,256]{2,1,0:T(8,128)}, u32[]{:S(2)}) copy-start(f32[1,1024,256]{2,1,0:T(8,128)} %param.7) | copy-start | bytes 3145732
  6.5 9.2 %copy-start.4 = (bf16[1,256,1024]{2,1,0:T(8,128)(2,1)S(1)}, bf16[1,256,1024]{2,1,0:T(8,128)(2,1)}, u32[]{:S(2)}) copy-start(bf16[1,256,1024]{2,1,0:T(8,128)(2,1)} %param.5) | copy-start | bytes 1572868
  15.7 1.3 copy-start.2
  15.7 1.9 %copy-start.3 = (f32[1024,1,512]{0,2,1:T(8,128)}, f32[1024,1,512]{0,2,1:T(8,128)S(1)}, u32[]{:S(2)}) copy-start(f32[1024,1,512]{0,2,1:T(8,128)S(1)} %get-tuple-element.6) | copy-start | bytes 6291460
  15.7 4.3 %copy-start.1 = (bf16[1024,256]{1,0:T(8,128)(2,1)S(1)}, bf16[1024,256]{1,0:T(8,128)(2,1)}, u32[]{:S(2)}) copy-start(bf16[1024,256]{1,0:T(8,128)(2,1)} %param.6) | copy-start | bytes 1572868
  17.6 12.3 %collective-permute-start.1 = (bf16[1,256,2,512]{1,3,2,0:T(8,128)(2,1)S(1)}, bf16[1,256,2,512]{1,3,2,0:T(8,128)(2,1)S(1)}, u32[]{:S(2)}, u32[]{:S(2)}) collective-permute-start(bf16[1,256,2,512]{1,3,2,0:T(8,128)(2,1)S(1)} %bitcast.80), channel_id=1, source_target_pairs={{0,1},{1,2},{2,3},{3,0},{4,5},{5,6},{6,7},{7,4},{8,9},{9,10},{10,1... | collective-permute-start | bytes 1572872 | tf_op jit(solution)/shard_map/ppermute | solution.py:16
  18.1 14.3 %collective-permute-start = (bf16[1,256,2,512]{1,3,2,0:T(8,128)(2,1)S(1)}, bf16[1,256,2,512]{1,3,2,0:T(8,128)(2,1)S(1)}, u32[]{:S(2)}, u32[]{:S(2)}) collective-permute-start(bf16[1,256,2,512]{1,3,2,0:T(8,128)(2,1)S(1)} %bitcast.81), channel_id=1, source_target_pairs={{0,3},{1,0},{2,1},{3,2},{4,7},{5,4},{6,5},{7,6},{8,11},{9,8},{10,9... | collective-permute-start | bytes 1572872 | tf_op jit(solution)/shard_map/ppermute | solution.py:18
  29.9 8.6 %collective-permute-start.2 = (bf16[1,256,2,512]{1,3,2,0:T(8,128)(2,1)S(1)}, bf16[1,256,2,512]{1,3,2,0:T(8,128)(2,1)S(1)}, u32[]{:S(2)}, u32[]{:S(2)}) collective-permute-start(bf16[1,256,2,512]{1,3,2,0:T(8,128)(2,1)S(1)} %collective-permute-done.1), channel_id=1, source_target_pairs={{0,1},{1,2},{2,3},{3,0},{4,5},{5,6},{6,7},{7,4},{8,9},{9,10},{10,1... | collective-permute-start | bytes 1572872 | tf_op jit(solution)/shard_map/ppermute | solution.py:16
  40.0 22.2 %all-to-all-start = ((bf16[1,1,256,2,512]{2,3,1,0,4:T(2,128)(2,1)}), bf16[1,1,256,2,512]{2,3,1,0,4:T(2,128)(2,1)S(1)}, u32[]{:S(2)}, u32[]{:S(2)}) async-start(bf16[1,1,256,2,512]{2,3,1,0,4:T(2,128)(2,1)} %copy.37), calls=%async_computation | async-start | bytes 1048576 | tf_op jit(solution)/shard_map/all_to_all | solution.py:56
  47.5 35.2 %reduce-scatter.2.cloned.1.call-start = ((), (), s32[]{:S(2)}) async-start(), calls=%async_computation.3 | async-start | bytes 327680 | tf_op jit(solution)/shard_map/reduce_scatter | solution.py:73
  64.3 74.7 %all-gather.2.cloned.1.call-start = ((), (), s32[]{:S(2)}) async-start(), calls=%async_computation.4 | async-start | bytes 2359296 | tf_op jit(solution)/shard_map/all_gather | solution.py:78
Sparse Core Ops, SparseCore 0:
  64.4 18.1 reduce-scatter.1
  89.9 49.0 all-gather.1
